TPU v7x, 32 devices: a whole 2x2x4 slice. The times are simulated.
32 devices in a mesh: rep: 4 (over x, core), fsdp: 4 (over z), tp: 2 (over y).
Axes of the slice: x: 2, y: 2, z: 4, core: 2. Of those that a mesh axis runs over, the one named last changes fastest.
Arguments:
- inputs: bfloat16 [512, 4096], P('rep', 'tp'), may hold values from -6 to 6
- out_grads: bfloat16 [512, 14336], P('rep', 'fsdp'), may hold values from -0.5 to 0.5
- error: bfloat16 [4, 4096, 14336], P('rep', 'tp', 'fsdp'), may hold values from -20 to 20
- q_init: bfloat16 [14336, 64], P('fsdp'), may hold values from -6 to 6
Outputs:
- new_error: bfloat16 [4, 4096, 14336], P('rep', 'tp', 'fsdp')
- p_factor: bfloat16 [4096, 64], P('tp')
- q_factor: bfloat16 [14336, 64], P('fsdp')
All inputs are finite; a program needn't handle non-finite values.
Results may differ from a plain program's by a relative error of at most 0.0014.
Values sent between devices are 32-bit elements; how exact they have to be, the bound alone decides.
A program may use at most 128 MiB of HBM per device.

v0:
```python
import math

import jax
import jax.numpy as jnp
from jax import lax
from jax.sharding import PartitionSpec as P

D = 4096
ITERS = 2


exact_mode = lax.Precision.HIGHEST


def inverse_factor(factor):
    identity = jnp.eye(factor.shape[0], dtype=jnp.float32)
    return jax.scipy.linalg.solve_triangular(factor, identity, lower=True)


def apply_inverse(inverse, matrix):
    return jnp.dot(matrix, inverse.T, precision=exact_mode)


def across(merged, left):
    return lax.dot_general(
        merged,
        left,
        (((0,), (0,)), ((), ())),
        precision=exact_mode,
        preferred_element_type=jnp.float32,
    )


def shards(inputs, out_grads, error, q_init):
    replicas = lax.axis_size("rep")
    merged = lax.dot_general(
        inputs, out_grads, (((0,), (0,)), ((), ())), preferred_element_type=jnp.float32
    )
    merged = merged + error[0].astype(jnp.float32)
    q_full = q_init.astype(jnp.float32)
    p_basis = jnp.zeros((merged.shape[0], q_full.shape[1]), jnp.float32)
    for iteration in range(ITERS):
        p_part = jnp.dot(merged, q_full, precision=exact_mode) / replicas
        p_full = lax.psum(p_part, ("rep", "fsdp"))
        gram_part = jnp.dot(p_full.T, p_full, precision=exact_mode)
        q_share = lax.psum_scatter(
            across(merged, p_full) / replicas, ("rep", "tp"), scatter_dimension=0, tiled=True
        )
        gram = lax.psum(gram_part, "tp")
        inverse = inverse_factor(jnp.linalg.cholesky(gram))
        p_basis = apply_inverse(inverse, p_full)
        q_full = lax.all_gather(apply_inverse(inverse, q_share), ("rep", "tp"), axis=0, tiled=True)
    approximation = jnp.dot(p_basis, q_full.T, precision=exact_mode)
    new_error = (merged - approximation).astype(jnp.bfloat16)[None]
    p_factor = (p_basis * math.sqrt(D)).astype(jnp.bfloat16)
    return (new_error, p_factor, q_full.astype(jnp.bfloat16))


def solution(mesh):
    in_specs = (P("rep", "tp"), P("rep", "fsdp"), P("rep", "tp", "fsdp"), P("fsdp", None))
    out_specs = (P("rep", "tp", "fsdp"), P("tp", None), P("fsdp", None))
    return jax.shard_map(shards, mesh=mesh, in_specs=in_specs, out_specs=out_specs, check_vma=False)
```

profile of v0, /device:TPU:0, one launch (start us, length us, event | category | flops | bytes accessed | tf_op | source)
XLA Modules:
  0.0 475.5 jit_solution(6352497552950826677)
XLA Ops:
  7.2 0.0 copy-start
  7.2 0.0 copy-start.4
  7.2 0.0 all-reduce.3.cloned.1.call-start
  7.2 1.1 copy-done
  8.4 14.9 %convert_add_fusion = f32[2048,3584]{1,0:T(8,128)} fusion(bf16[128,2048]{1,0:T(8,128)(2,1)} %param.7, bf16[128,3584]{1,0:T(8,128)(2,1)S(1)} %copy-done, bf16[1,2048,3584]{2,1,0:T(8,128)(2,1)} %param.9), kind=kOutput, calls=%fused_computation | convolution fusion | flops 1893728256 | bytes 45481984 | tf_op jit(solution)/shard_map/dot_general | solution.py:36
  23.2 0.0 copy-done.4
  23.2 19.9 %convolution_multiply_fusion.3 = f32[2048,64]{0,1:T(8,128)} fusion(f32[2048,3584]{1,0:T(8,128)} %convert_add_fusion, bf16[3584,64]{0,1:T(8,128)(2,1)S(1)} %copy-done.4), kind=kOutput, calls=%fused_computation.6 | convolution fusion | flops 5637275648 | bytes 30343168 | tf_op jit(solution)/shard_map/dot_general | solution.py:43
  43.1 0.0 all-reduce.3.cloned.1.call-update
  43.2 0.0 reduce-scatter.7.cloned.1.call-start
  43.2 93.5 %all-reduce.3.cloned.1.call-done = f32[2048,64]{0,1:T(8,128)} async-done(((f32[2048,64]{0,1:T(8,128)}), f32[2048,64]{0,1:T(8,128)}) %all-reduce.3.cloned.1.call-update) | async-done | bytes 524304 | tf_op jit(solution)/shard_map/psum | solution.py:44
  136.7 0.0 copy-start.3
  136.7 25.1 %convolution_multiply_fusion.1 = f32[3584,64]{0,1:T(8,128)S(1)} fusion(f32[2048,3584]{1,0:T(8,128)} %convert_add_fusion, f32[2048,64]{0,1:T(8,128)} %all-reduce.3.cloned.1.call-done), kind=kOutput, calls=%fused_computation.4 | convolution fusion | flops 5637373952 | bytes 30801920 | tf_op jit(solution)/shard_map/dot_general | solution.py:25
  161.8 1.8 copy.31
  163.6 0.0 reduce-scatter.7.cloned.1.call-update
  163.6 0.0 all-reduce.5.cloned.1.call-start
  163.7 0.0 copy-done.3
  163.7 0.6 fusion.11
  164.3 8.5 %psum.29 = f32[64,64]{0,1:T(8,128)S(1)} all-reduce(f32[64,64]{0,1:T(8,128)S(1)} %fusion.11), channel_id=1, replica_groups=mesh['rep'=4,'fsdp'=4,'tp'=2] {'tp'}, use_global_device_ids=true, to_apply=%region_2.0 | all-reduce | flops 4096 | bytes 32768 | tf_op jit(solution)/shard_map/psum | solution.py:49
  172.8 0.1 copy.24
  172.9 5.8 %cholesky.44 = f32[64,64]{1,0:T(8,128)S(1)} custom-call(f32[64,64]{1,0:T(8,128)S(1)} %fusion.10), custom_call_target="Cholesky" | custom-call | tf_op jit(solution)/shard_map/jit(cholesky)/cholesky | solution.py:50
  178.8 0.6 compare_reduce_fusion.1
  179.4 0.7 fusion.5
  180.1 4.9 %custom-call.6 = f32[1,64,64]{1,2,0:T(8,128)S(1)} custom-call(f32[1,64,64]{2,1,0:T(8,128)S(1)} %fusion.5), custom_call_target="InvertDiagBlocksLowerTriangular" | custom-call | tf_op jit(solution)/shard_map/jit(_solve_triangular)/triangular_solve | solution.py:17
  185.0 0.3 fusion.3
  185.2 18.7 %reduce-scatter.7.cloned.1.call-done = f32[448,64]{1,0:T(8,128)} async-done(((f32[3584,64]{1,0:T(8,128)}), f32[448,64]{1,0:T(8,128)}) %reduce-scatter.7.cloned.1.call-update) | async-done | bytes 114704
  203.9 1.4 convolution_bitcast_fusion.1
  205.3 19.7 %all-gather = f32[8,448,64]{1,2,0:T(8,128)S(1)} all-gather(f32[1,448,64]{1,2,0:T(8,128)S(1)} %convolution_bitcast_fusion.1), channel_id=1, replica_groups=mesh['rep'=4,'fsdp'=4,'tp'=2] {'rep','tp'}, dimensions={0}, use_global_device_ids=true | all-gather | bytes 1032192 | tf_op jit(solution)/shard_map/all_gather | solution.py:52
  224.9 0.6 copy.25
  225.5 0.4 reshape.18
  226.0 32.6 %convolution_multiply_fusion.2 = f32[2048,64]{0,1:T(8,128)} fusion(f32[2048,3584]{1,0:T(8,128)} %convert_add_fusion, f32[3584,64]{0,1:T(8,128)S(1)} %reshape.18), kind=kOutput, calls=%fused_computation.5 | convolution fusion | flops 5637275648 | bytes 30801920 | tf_op jit(solution)/shard_map/dot_general | solution.py:43
  258.6 0.0 all-reduce.5.cloned.1.call-update
  258.6 0.3 reduce-scatter.9.cloned.1.call-start
  258.9 90.9 %all-reduce.5.cloned.1.call-done = f32[2048,64]{0,1:T(8,128)} async-done(((f32[2048,64]{0,1:T(8,128)}), f32[2048,64]{0,1:T(8,128)}) %all-reduce.5.cloned.1.call-update) | async-done | bytes 524304 | tf_op jit(solution)/shard_map/psum | solution.py:44
  349.7 0.0 copy-start.2
  349.7 0.0 copy-start.1
  349.7 25.1 %convolution_multiply_fusion = f32[3584,64]{0,1:T(8,128)S(1)} fusion(f32[2048,3584]{1,0:T(8,128)} %convert_add_fusion, f32[2048,64]{0,1:T(8,128)} %all-reduce.5.cloned.1.call-done), kind=kOutput, calls=%fused_computation.3 | convolution fusion | flops 5637373952 | bytes 30801920 | tf_op jit(solution)/shard_map/dot_general | solution.py:25
  374.8 1.8 copy.33
  376.6 0.0 reduce-scatter.9.cloned.1.call-update
  376.6 0.0 copy-done.2
  376.6 0.6 fusion.12
  377.2 8.3 %psum.31 = f32[64,64]{0,1:T(8,128)S(1)} all-reduce(f32[64,64]{0,1:T(8,128)S(1)} %fusion.12), channel_id=1, replica_groups=mesh['rep'=4,'fsdp'=4,'tp'=2] {'tp'}, use_global_device_ids=true, to_apply=%region_6.9 | all-reduce | flops 4096 | bytes 32768 | tf_op jit(solution)/shard_map/psum | solution.py:49
  385.5 0.1 copy.27
  385.6 5.8 %cholesky.55 = f32[64,64]{1,0:T(8,128)S(1)} custom-call(f32[64,64]{1,0:T(8,128)S(1)} %fusion.8), custom_call_target="Cholesky" | custom-call | tf_op jit(solution)/shard_map/jit(cholesky)/cholesky | solution.py:50
  391.5 0.6 compare_reduce_fusion
  392.2 0.7 fusion.6
  392.8 4.9 %custom-call.7 = f32[1,64,64]{1,2,0:T(8,128)S(1)} custom-call(f32[1,64,64]{2,1,0:T(8,128)S(1)} %fusion.6), custom_call_target="InvertDiagBlocksLowerTriangular" | custom-call | tf_op jit(solution)/shard_map/jit(_solve_triangular)/triangular_solve | solution.py:17
  397.7 0.3 fusion.1
  398.0 1.3 multiply_convert_fusion
  399.3 17.6 %reduce-scatter.9.cloned.1.call-done = f32[448,64]{1,0:T(8,128)} async-done(((f32[3584,64]{1,0:T(8,128)}), f32[448,64]{1,0:T(8,128)}) %reduce-scatter.9.cloned.1.call-update) | async-done | bytes 114704
  416.9 1.4 convolution_bitcast_fusion
  418.3 19.9 %all-gather.1 = f32[8,448,64]{1,2,0:T(8,128)S(1)} all-gather(f32[1,448,64]{1,2,0:T(8,128)S(1)} %convolution_bitcast_fusion), channel_id=1, replica_groups=mesh['rep'=4,'fsdp'=4,'tp'=2] {'rep','tp'}, dimensions={0}, use_global_device_ids=true | all-gather | bytes 1032192 | tf_op jit(solution)/shard_map/all_gather | solution.py:52
  438.2 0.6 copy.28
  438.8 0.4 reshape.20
  439.2 0.8 convert_element_type.27
  440.0 28.9 %fusion = bf16[1,2048,3584]{2,1,0:T(8,128)(2,1)} fusion(f32[2048,3584]{1,0:T(8,128)} %convert_add_fusion, f32[2048,64]{0,1:T(8,128)S(1)} %get-tuple-element.6, f32[3584,64]{0,1:T(8,128)S(1)} %reshape.20), kind=kOutput, calls=%fused_computation.2 | convolution fusion | flops 5651824640 | bytes 45481984 | tf_op jit(solution)/shard_map/dot_general | solution.py:53
  469.0 0.0 copy-done.1
  (4 shorter events, 0.1 us)
Async XLA Ops:
  7.2 1.2 copy-start
  7.2 16.1 %copy-start.4 = (bf16[3584,64]{0,1:T(8,128)(2,1)S(1)}, bf16[3584,64]{0,1:T(8,128)(2,1)}, u32[]{:S(2)}) copy-start(bf16[3584,64]{0,1:T(8,128)(2,1)} %param.10) | copy-start | bytes 1376260
  7.2 129.5 %all-reduce.3.cloned.1.call-start = ((), (), s32[]{:S(2)}) async-start(), calls=%async_computation.2 | async-start | bytes 1048576 | tf_op jit(solution)/shard_map/psum | solution.py:44
  43.2 160.7 %reduce-scatter.7.cloned.1.call-start = ((), (), s32[]{:S(2)}) async-start(), calls=%async_computation.4 | async-start | bytes 2064384
  136.7 27.0 %copy-start.3 = (f32[2048,64]{0,1:T(8,128)S(1)}, f32[2048,64]{0,1:T(8,128)}, u32[]{:S(2)}) copy-start(f32[2048,64]{0,1:T(8,128)} %all-reduce.3.cloned.1.call-done) | copy-start | bytes 1572868
  163.6 186.1 %all-reduce.5.cloned.1.call-start = ((), (), s32[]{:S(2)}) async-start(), calls=%async_computation.3 | async-start | bytes 1048576 | tf_op jit(solution)/shard_map/psum | solution.py:44
  258.6 158.3 %reduce-scatter.9.cloned.1.call-start = ((), (), s32[]{:S(2)}) async-start(), calls=%async_computation.5 | async-start | bytes 2064384
  349.7 26.9 %copy-start.2 = (f32[2048,64]{0,1:T(8,128)S(1)}, f32[2048,64]{0,1:T(8,128)}, u32[]{:S(2)}) copy-start(f32[2048,64]{0,1:T(8,128)} %all-reduce.5.cloned.1.call-done) | copy-start | bytes 1572868
  349.7 119.3 %copy-start.1 = (bf16[128,3584]{1,0:T(8,128)(2,1)S(1)}, bf16[128,3584]{1,0:T(8,128)(2,1)}, u32[]{:S(2)}) copy-start(bf16[128,3584]{1,0:T(8,128)(2,1)} %param.8) | copy-start | bytes 2752516
Sparse Core Ops, SparseCore 0:
  43.3 93.4 all-reduce.2
  163.8 40.0 reduce-scatter.6
  258.7 90.9 all-reduce.4
  376.8 40.0 reduce-scatter.8
where the time goes:
time: 476 us
  waiting for transfers between devices  221 us (46%)
  matrix products  152 us (32%)
  blocking collectives  56.4 us (12%)
  other arithmetic  25 us (5%)
  between operations  13.9 us (3%)
  local copies, waits for them, and re-layouts  6.87 us (1%)
    psum x2, waiting for transfers between devices, shards(): p_full = lax.psum(p_part, ('rep', 'fsdp'))  184 us
    dot_general x2, matrix products, shards(): p_part = jnp.dot(merged, q_full, precision=exact_mode) / replicas  52.5 us
    dot_general x2, matrix products, across(): lax.dot_general(merged, left, (((0,), (0,)), ((), ())), precision=exact_m...  50.2 us
    all_gather x2, blocking collectives, shards(): lax.all_gather(apply_inverse(inverse, q_share), ('rep', 'tp'), axis=0, ti...  39.6 us
    unnamed x6, waiting for transfers between devices  36.3 us
    dot_general x1, matrix products, shards(): approximation = jnp.dot(p_basis, q_full.T, precision=exact_mode)  28.9 us
    psum x2, blocking collectives, shards(): gram = lax.psum(gram_part, 'tp')  16.8 us
    dot_general x1, matrix products, shards(): lax.dot_general(inputs, out_grads, (((0,), (0,)), ((), ())), preferred_el...  14.9 us
  transfers between devices with their start and end apart: 4, of which 4 were waited for; matrix products, arithmetic and copies ran while one was open for 6% of the time, Pallas kernels for 0%

commit v1 on v0

v1 whole, which is shorter than its diff:
```python
import functools
import math

import jax
import jax.numpy as jnp
from jax import lax
from jax.experimental import pallas as pl
from jax.experimental.pallas import tpu as pltpu
from jax.sharding import PartitionSpec as P

ITERS = 2
PIECES = 3
exact_mode = lax.Precision.HIGHEST
MESH = pl.DeviceIdType.MESH


def contract(left, right, at_left, at_right, precision=None):
    return lax.dot_general(
        left,
        right,
        (((at_left,), (at_right,)), ((), ())),
        precision=precision,
        preferred_element_type=jnp.float32,
    )


def pieces_of(value):
    pieces = []
    for _ in range(PIECES):
        piece = value.astype(jnp.bfloat16)
        pieces.append(piece)
        value = value - piece.astype(jnp.float32)
    return jnp.concatenate(pieces, axis=0)


def fold(stacked, rank):
    total = stacked[:rank]
    for at in range(rank, stacked.shape[0], rank):
        total = total + stacked[at : at + rank]
    return total


class Group:
    def __init__(self, axes, sizes):
        self.axes, self.sizes = axes, sizes
        self.count = sizes[0] * sizes[1]

    def me(self):
        return lax.axis_index(self.axes[0]) * self.sizes[1] + lax.axis_index(self.axes[1])

    def peer(self, step):
        at = lax.rem(self.me() + step, self.count)
        return at, {
            self.axes[0]: lax.div(at, self.sizes[1]),
            self.axes[1]: lax.rem(at, self.sizes[1]),
        }

    def meet(self):
        barrier = pltpu.get_barrier_semaphore()
        for step in range(1, self.count):
            pl.semaphore_signal(barrier, inc=1, device_id=self.peer(step)[1], device_id_type=MESH)
        pl.semaphore_wait(barrier, self.count - 1)

    def scatter(self, part_of, slots, send, recv):
        copies = []
        for step in range(1, self.count):
            at, device = self.peer(step)
            copies.append(
                pltpu.make_async_remote_copy(
                    part_of(at), slots.at[step - 1], send.at[step - 1], recv.at[step - 1],
                    device_id=device, device_id_type=MESH,
                )
            )
            copies[-1].start()
        return copies

    def share(self, part, send, recv):
        copies = []
        for step in range(1, self.count):
            _, device = self.peer(step)
            copies.append(
                pltpu.make_async_remote_copy(
                    part, part, send.at[step - 1], recv.at[step - 1],
                    device_id=device, device_id_type=MESH,
                )
            )
            copies[-1].start()
        return copies


def left_kernel(group, replicas, a_ref, q_ref, x_ref, g_ref, p_ref, p3_ref,
                total, slots, send, recv, send2, recv2):
    rank, columns = p_ref.shape
    width = columns // group.count
    inner = fold(contract(q_ref[...], g_ref[...], 1, 1), rank)
    outer = fold(contract(pieces_of(inner), x_ref[...], 1, 0), rank)
    total[...] = (outer + fold(a_ref[...], rank)) / replicas
    group.meet()

    def part(ref, at):
        return ref.at[:, pl.ds(pl.multiple_of(at * width, width), width)]

    copies = group.scatter(lambda at: part(total, at), slots, send, recv)
    mine = part(total, group.me())[...]
    for step, copy in enumerate(copies):
        copy.wait_recv()
        mine = mine + slots[step]
    part(p_ref, group.me())[...] = mine
    shared = group.share(part(p_ref, group.me()), send2, recv2)
    for copy in copies:
        copy.wait_send()
    for copy in shared:
        copy.wait()
    p3_ref[...] = pieces_of(p_ref[...])


def invert_into(grid, inverse):
    rank = grid.shape[0]
    lane = lax.broadcasted_iota(jnp.int32, grid.shape, 1)
    row_at = lax.broadcasted_iota(jnp.int32, (rank, 1), 0)

    def eliminate(j, carry):
        row = grid[pl.ds(j, 1), :]
        now = grid[...]
        column = jnp.sum(jnp.where(lane == rank + j, now, 0.0), axis=1, keepdims=True)
        pivot = jnp.sum(jnp.where(lane[:1] == rank + j, row, 0.0), axis=1, keepdims=True)
        inverse[pl.ds(j, 1), :] = row / jnp.sqrt(pivot)
        factor = jnp.where(row_at > j, column / pivot, 0.0)
        grid[...] = now - factor * row
        return carry

    lax.fori_loop(0, rank, eliminate, 0)


def right_kernel(group, pairs, replicas, a_ref, p_ref, p3_ref, x_ref, g_ref,
                 q_ref, q3_ref, basis_ref,
                 total, gathered, slots, mine_gram, gram_slots, grid, inverse,
                 send, recv, send2, recv2, gram_send, gram_recv):
    rank, columns = q_ref.shape
    height = rank // group.count
    inner = fold(contract(p3_ref[...], x_ref[...], 1, 1), rank)
    outer = fold(contract(pieces_of(inner), g_ref[...], 1, 0), rank)
    total[...] = (outer + fold(a_ref[...], rank)) / replicas
    left = p_ref[...]
    mine_gram[...] = contract(left, jnp.concatenate([left, left], axis=0), 1, 1, exact_mode)
    group.meet()

    def part(ref, at):
        return ref.at[pl.ds(pl.multiple_of(at * height, height), height), :]

    gram_copies = []
    for step in range(1, pairs):
        target = lax.rem(lax.axis_index("tp") + step, pairs)
        gram_copies.append(
            pltpu.make_async_remote_copy(
                mine_gram, gram_slots.at[step - 1], gram_send.at[step - 1], gram_recv.at[step - 1],
                device_id={"tp": target}, device_id_type=MESH,
            )
        )
        gram_copies[-1].start()
    copies = group.scatter(lambda at: part(total, at), slots, send, recv)
    gram = mine_gram[...]
    for step, copy in enumerate(gram_copies):
        copy.wait()
        gram = gram + gram_slots[step]
    lane = lax.broadcasted_iota(jnp.int32, gram.shape, 1)
    row_at = lax.broadcasted_iota(jnp.int32, gram.shape, 0)
    grid[...] = jnp.where(lane < rank, jnp.where(lane == row_at, 1.0, 0.0), gram)
    mine = part(total, group.me())[...]
    for step, copy in enumerate(copies):
        copy.wait_recv()
        mine = mine + slots[step]
    part(gathered, group.me())[...] = mine
    shared = group.share(part(gathered, group.me()), send2, recv2)
    invert_into(grid, inverse)
    for copy in copies:
        copy.wait_send()
    lower = inverse[:, :rank]
    basis_ref[...] = contract(lower, left, 1, 0, exact_mode)
    for copy in shared:
        copy.wait()
    result = contract(lower, gathered[...], 1, 0, exact_mode)
    q_ref[...] = result
    q3_ref[...] = pieces_of(result)


def vmem(count):
    return [pl.BlockSpec(memory_space=pltpu.VMEM)] * count


def dma(count):
    return pltpu.SemaphoreType.DMA((count,))


def left_call(tag, group, replicas, rank, a, q3, inputs, out_grads):
    columns = a.shape[1]
    width = columns // group.count
    others = group.count - 1
    return pl.pallas_call(
        functools.partial(left_kernel, group, replicas),
        name="left_reduce",
        out_shape=(
            jax.ShapeDtypeStruct((rank, columns), jnp.float32),
            jax.ShapeDtypeStruct((PIECES * rank, columns), jnp.bfloat16),
        ),
        in_specs=vmem(4),
        out_specs=vmem(2),
        scratch_shapes=[
            pltpu.VMEM((rank, columns), jnp.float32),
            pltpu.VMEM((others, rank, width), jnp.float32),
            dma(others), dma(others), dma(others), dma(others),
        ],
        compiler_params=pltpu.CompilerParams(collective_id=tag, has_side_effects=True, vmem_limit_bytes=40 << 20),
    )(a, q3, inputs, out_grads)


def right_call(group, pairs, replicas, rank, a, p, p3, inputs, out_grads):
    columns = a.shape[1]
    height = rank // group.count
    others = group.count - 1
    return pl.pallas_call(
        functools.partial(right_kernel, group, pairs, replicas),
        name="right_reduce",
        out_shape=(
            jax.ShapeDtypeStruct((rank, columns), jnp.float32),
            jax.ShapeDtypeStruct((PIECES * rank, columns), jnp.bfloat16),
            jax.ShapeDtypeStruct(p.shape, jnp.float32),
        ),
        in_specs=vmem(5),
        out_specs=vmem(3),
        scratch_shapes=[
            pltpu.VMEM((rank, columns), jnp.float32),
            pltpu.VMEM((rank, columns), jnp.float32),
            pltpu.VMEM((others, height, columns), jnp.float32),
            pltpu.VMEM((rank, 2 * rank), jnp.float32),
            pltpu.VMEM((pairs - 1, rank, 2 * rank), jnp.float32),
            pltpu.VMEM((rank, 2 * rank), jnp.float32),
            pltpu.VMEM((rank, 2 * rank), jnp.float32),
            dma(others), dma(others), dma(others), dma(others), dma(pairs - 1), dma(pairs - 1),
        ],
        compiler_params=pltpu.CompilerParams(collective_id=ITERS, has_side_effects=True, vmem_limit_bytes=40 << 20),
    )(a, p, p3, inputs, out_grads)


def rounded_pieces(value):
    pieces = []
    for _ in range(PIECES):
        piece = lax.reduce_precision(value, 8, 7)
        pieces.append(piece.astype(jnp.bfloat16))
        value = value - piece
    return jnp.concatenate(pieces, axis=0)


def plain_left(replicas, rank, a, q3, inputs, out_grads):
    inner = fold(contract(q3, out_grads, 1, 1), rank)
    outer = fold(contract(rounded_pieces(inner), inputs, 1, 0), rank)
    p = lax.psum((outer + fold(a, rank)) / replicas, ("rep", "fsdp"))
    return p, rounded_pieces(p)


def plain_right(replicas, rank, a, p, p3, inputs, out_grads):
    inner = fold(contract(p3, inputs, 1, 1), rank)
    outer = fold(contract(rounded_pieces(inner), out_grads, 1, 0), rank)
    q = lax.psum((outer + fold(a, rank)) / replicas, ("rep", "tp"))
    gram = lax.psum(contract(p, p, 1, 1, exact_mode), "tp")
    inverse = jax.scipy.linalg.solve_triangular(
        jnp.linalg.cholesky(gram), jnp.eye(rank, dtype=jnp.float32), lower=True
    )
    q = contract(inverse, q, 1, 0, exact_mode)
    return q, rounded_pieces(q), contract(inverse, p, 1, 0, exact_mode)


def shards(inputs, out_grads, error, q_init):
    replicas, splits, pairs = lax.axis_size("rep"), lax.axis_size("fsdp"), lax.axis_size("tp")
    rank = q_init.shape[1]
    rows, columns = error.shape[1:]
    left_group = Group(("rep", "fsdp"), (replicas, splits))
    right_group = Group(("rep", "tp"), (replicas, pairs))
    own_left = rows % (left_group.count * 128) == 0 and left_group.count > 1
    own_right = rank % (right_group.count * 8) == 0 and pairs > 1 and rank == 64
    error = error[0]
    q3 = q_init.T
    for iteration in range(ITERS):
        a = contract(q3, error, 1, 1)
        if own_left:
            p, p3 = left_call(iteration, left_group, replicas, rank, a, q3, inputs, out_grads)
        else:
            p, p3 = plain_left(replicas, rank, a, q3, inputs, out_grads)
        a = contract(p3, error, 1, 0)
        if own_right:
            q, q3, basis = right_call(right_group, pairs, replicas, rank, a, p, p3, inputs, out_grads)
        else:
            q, q3, basis = plain_right(replicas, rank, a, p, p3, inputs, out_grads)
    basis3 = rounded_pieces(-basis)
    high, low = basis3[:rank], basis3[rank : 2 * rank]
    lefts = jnp.concatenate([inputs, high, high, low], axis=0)
    rights = jnp.concatenate([out_grads, q3[:rank], q3[rank : 2 * rank], q3[:rank]], axis=0)
    merged = contract(lefts, rights, 0, 0) + error.astype(jnp.float32)
    p_factor = (basis * math.sqrt(rows * pairs)).astype(jnp.bfloat16).T
    return (merged.astype(jnp.bfloat16)[None], p_factor, q.astype(jnp.bfloat16).T)


def solution(mesh):
    in_specs = (P("rep", "tp"), P("rep", "fsdp"), P("rep", "tp", "fsdp"), P("fsdp", None))
    out_specs = (P("rep", "tp", "fsdp"), P("tp", None), P("fsdp", None))
    return jax.shard_map(shards, mesh=mesh, in_specs=in_specs, out_specs=out_specs, check_vma=False)
```

time: 476 us -> 170 us (0.36)
  waiting for transfers between devices: 221 us -> 0 us
  Pallas kernels: 0 us -> 122 us
  matrix products: 152 us -> 46.1 us
  blocking collectives: 56.4 us -> 0 us
  other arithmetic: 25 us -> 1.64 us
  between operations: 13.9 us -> 0.75 us
  local copies, waits for them, and re-layouts: 6.87 us -> 0.1 us
    psum x2 -> x0, waiting for transfers between devices: 184 us -> none  [shards(): p_full = lax.psum(p_part, ('rep', 'fsdp'))]
    pallas_call x0 -> x4, Pallas kernels: none -> 122 us  [the longest x2 63.6 us: left_call(): pl.pallas_call(functools.partial(left_kernel, group, replicas), name='lef...]
    dot_general x11 -> x5, matrix products: 152 us -> 46.1 us  [contract(): lax.dot_general(left, right, (((at_left,), (at_right,)), ((), ())), preci...]
    all_gather x2 -> x0, blocking collectives: 39.6 us -> none  [shards(): lax.all_gather(apply_inverse(inverse, q_share), ('rep', 'tp'), axis=0, ti...]
    unnamed x6 -> x0, waiting for transfers between devices: 36.3 us -> none
    another operation x10 -> x0, other arithmetic: 24.1 us -> none  [the longest x6 13 us: shards(): inverse = inverse_factor(jnp.linalg.cholesky(gram))]
    psum x2 -> x0, blocking collectives: 16.8 us -> none  [shards(): gram = lax.psum(gram_part, 'tp')]
    unnamed x14 -> x6, local copies, waits for them, and re-layouts: 5.5 us -> 0.01 us
  transfers between devices with their start and end apart: 4 -> 0, of which waited for: 4 -> 0; matrix products, arithmetic and copies ran while one was open for 6% -> 0% of each run, Pallas kernels for 0% -> 0%
where the time goes in v1:
time: 170 us
  Pallas kernels  122 us (72%)
  matrix products  46.1 us (27%)
    pallas_call x2, Pallas kernels, left_call(): pl.pallas_call(functools.partial(left_kernel, group, replicas), name='lef...  63.6 us
    pallas_call x2, Pallas kernels, right_call(): pl.pallas_call(functools.partial(right_kernel, group, pairs, replicas), n...  58.1 us
    dot_general x5, matrix products, contract(): lax.dot_general(left, right, (((at_left,), (at_right,)), ((), ())), preci...  46.1 us

profile of v1, /device:TPU:0, one launch (start us, length us, event | category | flops | bytes accessed | tf_op | source)
XLA Modules:
  0.0 170.3 jit_solution(15425903323864206300)
XLA Ops:
  0.6 0.0 copy-start
  0.6 0.0 copy-start.1
  0.7 0.0 copy-start.2
  0.7 9.9 %fusion.6.a_ref = f32[64,2048]{1,0:T(8,128)S(1)} fusion(bf16[3584,64]{0,1:T(8,128)(2,1)} %param.7, bf16[1,2048,3584]{2,1,0:T(8,128)(2,1)} %param.6), kind=kOutput, calls=%fused_computation.7 | convolution fusion | flops 939524096 | bytes 15663104 | tf_op jit(solution)/shard_map/dot_general | solution.py:18
  10.6 0.0 copy-done
  10.6 0.0 copy-done.1
  10.6 0.0 copy-done.2
  10.6 33.0 %left_reduce.2 = (f32[64,2048]{1,0:T(8,128)S(1)}, bf16[192,2048]{1,0:T(8,128)(2,1)S(1)}) custom-call(f32[64,2048]{1,0:T(8,128)S(1)} %fusion.6.a_ref, bf16[64,3584]{1,0:T(8,128)(2,1)S(1)} %bitcast.23, bf16[128,2048]{1,0:T(8,128)(2,1)S(1)} %copy-done.1, bf16[128,3584]{1,0:T(8,128)(2,1)S(1)} %copy-done), custom_call_target="tpu_custom_call" | custom-call | tf_op jit(solution)/shard_map/left_reduce/pallas_call | solution.py:199
  43.7 7.0 %fusion.4.a_ref = f32[192,3584]{1,0:T(8,128)S(1)} fusion(bf16[192,2048]{1,0:T(8,128)(2,1)S(1)} %get-tuple-element.11.p3_ref, bf16[1,2048,3584]{2,1,0:T(8,128)(2,1)} %param.6), kind=kOutput, calls=%fused_computation.5 | convolution fusion | flops 2818572288 | bytes 18219008 | tf_op jit(solution)/shard_map/dot_general | solution.py:18
  50.6 29.0 %right_reduce.2 = (f32[64,3584]{1,0:T(8,128)}, bf16[192,3584]{1,0:T(8,128)(2,1)S(1)}, f32[64,2048]{1,0:T(8,128)}) custom-call(f32[192,3584]{1,0:T(8,128)S(1)} %fusion.4.a_ref, f32[64,2048]{1,0:T(8,128)S(1)} %get-tuple-element.12.p_ref, bf16[192,2048]{1,0:T(8,128)(2,1)S(1)} %get-tuple-element.11.p3_ref, bf16[128,2048]{1,0:T(8,128)(2,1)S(1)} %copy-done.1, ...), custom_call_target="tpu_custom_call" | custom-call | tf_op jit(solution)/shard_map/right_reduce/pallas_call | solution.py:221
  79.7 8.2 %fusion.2.a_ref = f32[192,2048]{1,0:T(8,128)S(1)} fusion(bf16[192,3584]{1,0:T(8,128)(2,1)S(1)} %get-tuple-element.13.q_ref, bf16[1,2048,3584]{2,1,0:T(8,128)(2,1)} %param.6), kind=kOutput, calls=%fused_computation.3 | convolution fusion | flops 2818572288 | bytes 17629184 | tf_op jit(solution)/shard_map/dot_general | solution.py:18
  87.8 30.6 %left_reduce.3 = (f32[64,2048]{1,0:T(8,128)S(1)}, bf16[192,2048]{1,0:T(8,128)(2,1)S(1)}) custom-call(f32[192,2048]{1,0:T(8,128)S(1)} %fusion.2.a_ref, bf16[192,3584]{1,0:T(8,128)(2,1)S(1)} %get-tuple-element.13.q_ref, bf16[128,2048]{1,0:T(8,128)(2,1)S(1)} %copy-done.1, bf16[128,3584]{1,0:T(8,128)(2,1)S(1)} %copy-done), custom_call_target="tpu_custom_call" | custom-call | tf_op jit(solution)/shard_map/left_reduce/pallas_call | solution.py:199
  118.4 6.8 %fusion.a_ref = f32[192,3584]{1,0:T(8,128)S(1)} fusion(bf16[192,2048]{1,0:T(8,128)(2,1)S(1)} %get-tuple-element.14.p3_ref, bf16[1,2048,3584]{2,1,0:T(8,128)(2,1)} %param.6), kind=kOutput, calls=%fused_computation.1 | convolution fusion | flops 2818572288 | bytes 18219008 | tf_op jit(solution)/shard_map/dot_general | solution.py:18
  125.2 29.1 %right_reduce.3 = (f32[64,3584]{1,0:T(8,128)S(1)}, bf16[192,3584]{1,0:T(8,128)(2,1)S(1)}, f32[64,2048]{1,0:T(8,128)S(1)}) custom-call(f32[192,3584]{1,0:T(8,128)S(1)} %fusion.a_ref, f32[64,2048]{1,0:T(8,128)S(1)} %get-tuple-element.15.p_ref, bf16[192,2048]{1,0:T(8,128)(2,1)S(1)} %get-tuple-element.14.p3_ref, bf16[128,2048]{1,0:T(8,128)(2,1)S(1)} %copy-done.1, ...), custom_call_target="tpu_custom_call" | custom-call | tf_op jit(solution)/shard_map/right_reduce/pallas_call | solution.py:221
  154.3 0.8 fusion.23
  155.2 0.8 convert_bitcast_fusion
  156.0 0.1 slice.8
  156.1 14.2 %fusion.8 = bf16[1,2048,3584]{2,1,0:T(8,128)(2,1)} fusion(bf16[1,2048,3584]{2,1,0:T(8,128)(2,1)} %param.6, bf16[64,3584]{1,0:T(8,128)(2,1)S(1)} %slice.9, bf16[128,3584]{1,0:T(8,128)(2,1)S(1)} %slice.8, bf16[128,3584]{1,0:T(8,128)(2,1)S(1)} %copy-done, bf16[64,2048]{1,0:T(8,128)(2,1)S(1)} %get-tuple-element.20, bf16[64,2048]{1,0:T(8,128)(2,1)S(1)} %get-tuple-element.21, ...), kind=kOutput, calls=%fused_computation.9 | convolution fusion | flops 4731764736 | bytes 32702464 | tf_op jit(solution)/shard_map/dot_general | solution.py:18
  (1 shorter events, 0.0 us)
Async XLA Ops:
  0.6 10.0 %copy-start = (bf16[128,3584]{1,0:T(8,128)(2,1)S(1)}, bf16[128,3584]{1,0:T(8,128)(2,1)}, u32[]{:S(2)}) copy-start(bf16[128,3584]{1,0:T(8,128)(2,1)} %g_ref.7) | copy-start | bytes 2752516
  0.6 10.0 %copy-start.1 = (bf16[128,2048]{1,0:T(8,128)(2,1)S(1)}, bf16[128,2048]{1,0:T(8,128)(2,1)}, u32[]{:S(2)}) copy-start(bf16[128,2048]{1,0:T(8,128)(2,1)} %x_ref.7) | copy-start | bytes 1572868
  0.7 10.0 %copy-start.2 = (bf16[3584,64]{0,1:T(8,128)(2,1)S(1)}, bf16[3584,64]{0,1:T(8,128)(2,1)}, u32[]{:S(2)}) copy-start(bf16[3584,64]{0,1:T(8,128)(2,1)} %param.7) | copy-start | bytes 1376260

commit v2 on v1

v2 whole, which is shorter than its diff:
```python
import functools
import math

import jax
import jax.numpy as jnp
from jax import lax
from jax.experimental import pallas as pl
from jax.experimental.pallas import tpu as pltpu
from jax.sharding import PartitionSpec as P

ITERS = 2
PIECES = 3
BLOCK = 512
exact_mode = lax.Precision.HIGHEST
MESH = pl.DeviceIdType.MESH


def contract(left, right, at_left, at_right, precision=None):
    return lax.dot_general(
        left,
        right,
        (((at_left,), (at_right,)), ((), ())),
        precision=precision,
        preferred_element_type=jnp.float32,
    )


def pieces_of(value):
    pieces = []
    for _ in range(PIECES):
        piece = value.astype(jnp.bfloat16)
        pieces.append(piece)
        value = value - piece.astype(jnp.float32)
    return jnp.concatenate(pieces, axis=0)


def fold(stacked, rank):
    total = stacked[:rank]
    for at in range(rank, stacked.shape[0], rank):
        total = total + stacked[at : at + rank]
    return total


class Group:
    def __init__(self, axis, replicas, size):
        self.axis, self.size = axis, size
        self.count = (replicas // 2) * size

    def core(self):
        return lax.rem(lax.axis_index("rep"), 2)

    def me(self):
        return lax.div(lax.axis_index("rep"), 2) * self.size + lax.axis_index(self.axis)

    def at(self, step):
        return lax.rem(self.me() + step, self.count)

    def device(self, step):
        at = self.at(step)
        return {"rep": 2 * lax.div(at, self.size) + self.core(), self.axis: lax.rem(at, self.size)}

    def partner(self):
        return {"rep": lax.axis_index("rep") + 1 - 2 * self.core()}

    def greet(self):
        barrier = pltpu.get_barrier_semaphore()
        pl.semaphore_signal(barrier, inc=1, device_id=self.partner(), device_id_type=MESH)
        for step in range(1, self.count):
            pl.semaphore_signal(barrier, inc=1, device_id=self.device(step), device_id_type=MESH)

    def meet(self):
        pl.semaphore_wait(pltpu.get_barrier_semaphore(), self.count)


def push(source, target, sems, at, device):
    copy = pltpu.make_async_remote_copy(
        source, target, sems.at[0, at], sems.at[1, at], device_id=device, device_id_type=MESH
    )
    copy.start()
    return copy


def aligned(at, size):
    return pl.ds(pl.multiple_of(at * size, size), size)


def gather(group, part_of, share_sems, pass_sems):
    own = part_of(group.me())
    passed = [push(own, own, pass_sems, 0, group.partner())]
    shared = [
        push(own, own, share_sems, step - 1, group.device(step)) for step in range(1, group.count)
    ]

    def finish():
        for step in range(1, group.count):
            shared[step - 1].wait_recv()
            part = part_of(group.at(group.count - step))
            passed.append(push(part, part, pass_sems, step, group.partner()))
        for copy in shared:
            copy.wait_send()
        for copy in passed:
            copy.wait()

    return finish


def left_kernel(group, replicas, q_ref, x_ref, g_ref, e_ref, p_ref, p3_ref,
                held, total, outgoing, core_slots, slots,
                load_sems, core_sems, send_sems, share_sems, pass_sems):
    rank, columns = p_ref.shape
    count = group.count
    width, half = columns // count, rank // 2
    mine_rows, other_rows = aligned(group.core(), half), aligned(1 - group.core(), half)
    order = list(range(1, count)) + [0]
    loads = {}
    for step in order:
        rows = aligned(group.at(step), width)
        loads[step] = pltpu.make_async_copy(e_ref.at[0, rows, :], held.at[rows, :], load_sems.at[step])
        loads[step].start()
    group.greet()
    inner = fold(contract(q_ref[...], g_ref[...], 1, 1), rank)
    total[...] = fold(contract(pieces_of(inner), x_ref[...], 1, 0), rank)
    group.meet()
    core_copies, copies = {}, []

    def forward(step):
        core_copies[step].wait_recv()
        value = total[mine_rows, aligned(group.at(step), width)] + core_slots[step]
        if step == 0:
            return value
        outgoing[step - 1] = value
        copies.append(
            push(outgoing.at[step - 1], slots.at[step - 1], send_sems, step - 1, group.device(step))
        )

    for place, step in enumerate(order):
        span = aligned(group.at(step), width)
        loads[step].wait()
        product = fold(contract(q_ref[...], held[span, :], 1, 1), rank)
        total[:, span] = (total[:, span] + product) / replicas
        core_copies[step] = push(
            total.at[other_rows, span], core_slots.at[step], core_sems, step, group.partner()
        )
        if place:
            forward(order[place - 1])
    mine = forward(0)
    for step in range(1, count):
        copies[step - 1].wait_recv()
        mine = mine + slots[step - 1]
    p_ref[mine_rows, aligned(group.me(), width)] = mine
    finish = gather(
        group, lambda at: p_ref.at[mine_rows, aligned(at, width)], share_sems, pass_sems
    )
    for copy in copies:
        copy.wait_send()
    for step in order:
        core_copies[step].wait_send()
    finish()
    p3_ref[...] = pieces_of(p_ref[...])


def invert_into(grid, inverse):
    rank = grid.shape[0]
    lane = lax.broadcasted_iota(jnp.int32, grid.shape, 1)
    row_at = lax.broadcasted_iota(jnp.int32, (rank, 1), 0)

    def eliminate(j, carry):
        row = grid[pl.ds(j, 1), :]
        now = grid[...]
        column = jnp.sum(jnp.where(lane == rank + j, now, 0.0), axis=1, keepdims=True)
        pivot = jnp.sum(jnp.where(lane[:1] == rank + j, row, 0.0), axis=1, keepdims=True)
        inverse[pl.ds(j, 1), :] = row / jnp.sqrt(pivot)
        factor = jnp.where(row_at > j, column / pivot, 0.0)
        grid[...] = now - factor * row
        return carry

    lax.fori_loop(0, rank, eliminate, 0)


def right_kernel(group, pairs, replicas, p_ref, p3_ref, x_ref, g_ref, e_ref,
                 q_ref, q3_ref, basis_ref,
                 held, total, summed, gathered, core_slots, slots, own_gram, gram_slots, grid, inverse,
                 load_sems, core_sems, send_sems, share_sems, pass_sems, gram_sems):
    rank, columns = q_ref.shape
    count = group.count
    half, height = rank // 2, rank // 2 // count
    blocks, _, width = core_slots.shape
    mine_rows, other_rows = aligned(group.core(), half), aligned(1 - group.core(), half)
    loads = []
    for block in range(blocks):
        span = pl.ds(block * width, width)
        loads.append(
            pltpu.make_async_copy(e_ref.at[0, :, span], held.at[:, span], load_sems.at[block])
        )
        loads[-1].start()
    group.greet()
    inner = fold(contract(p3_ref[...], x_ref[...], 1, 1), rank)
    total[...] = fold(contract(pieces_of(inner), g_ref[...], 1, 0), rank)
    left = p_ref[...]
    own_gram[...] = contract(left, jnp.concatenate([left, left], axis=0), 1, 1, exact_mode)
    group.meet()
    gram_copies = []
    for step in range(1, pairs):
        target = lax.rem(lax.axis_index("tp") + step, pairs)
        gram_copies.append(
            push(own_gram, gram_slots.at[step - 1], gram_sems, step - 1, {"tp": target})
        )
    core_copies, copies = [], []

    def forward(block):
        span = pl.ds(block * width, width)
        core_copies[block].wait_recv()
        summed[:, span] = total[mine_rows, span] + core_slots[block]
        for step in range(1, count):
            copies.append(
                push(
                    summed.at[aligned(group.at(step), height), span],
                    slots.at[step - 1, :, span],
                    send_sems,
                    block * (count - 1) + step - 1,
                    group.device(step),
                )
            )

    for block in range(blocks):
        span = pl.ds(block * width, width)
        loads[block].wait()
        product = fold(contract(p3_ref[...], held[:, span], 1, 0), rank)
        total[:, span] = (total[:, span] + product) / replicas
        core_copies.append(
            push(total.at[other_rows, span], core_slots.at[block], core_sems, block, group.partner())
        )
        if block:
            forward(block - 1)
    forward(blocks - 1)
    gram = own_gram[...]
    for step, copy in enumerate(gram_copies):
        copy.wait()
        gram = gram + gram_slots[step]
    lane = lax.broadcasted_iota(jnp.int32, gram.shape, 1)
    row_at = lax.broadcasted_iota(jnp.int32, gram.shape, 0)
    grid[...] = jnp.where(lane < rank, jnp.where(lane == row_at, 1.0, 0.0), gram)

    def own_part(at):
        return gathered.at[aligned(group.core() * count + at, height), :]

    mine = summed[aligned(group.me(), height), :]
    for copy in copies:
        copy.wait_recv()
    for step in range(1, count):
        mine = mine + slots[step - 1]
    own_part(group.me())[...] = mine
    finish = gather(group, own_part, share_sems, pass_sems)
    invert_into(grid, inverse)
    lower = inverse[:, :rank]
    basis_ref[...] = contract(lower, left, 1, 0, exact_mode)
    for copy in copies + core_copies:
        copy.wait_send()
    finish()
    result = contract(lower, gathered[...], 1, 0, exact_mode)
    q_ref[...] = result
    q3_ref[...] = pieces_of(result)


def in_places():
    return [pl.BlockSpec(memory_space=pltpu.VMEM)] * 3 + [pl.BlockSpec(memory_space=pl.ANY)]


def dma(count):
    return pltpu.SemaphoreType.DMA((2, count))


def params(tag):
    return pltpu.CompilerParams(collective_id=tag, has_side_effects=True, vmem_limit_bytes=58 << 20)


def left_call(tag, group, replicas, rank, q3, inputs, out_grads, error):
    rows, columns = error.shape[1:]
    count, half = group.count, rank // 2
    width = rows // count
    return pl.pallas_call(
        functools.partial(left_kernel, group, replicas),
        name="left_reduce",
        out_shape=(
            jax.ShapeDtypeStruct((rank, rows), jnp.float32),
            jax.ShapeDtypeStruct((PIECES * rank, rows), jnp.bfloat16),
        ),
        in_specs=in_places(),
        out_specs=[pl.BlockSpec(memory_space=pltpu.VMEM)] * 2,
        scratch_shapes=[
            pltpu.VMEM((rows, columns), jnp.bfloat16),
            pltpu.VMEM((rank, rows), jnp.float32),
            pltpu.VMEM((count - 1, half, width), jnp.float32),
            pltpu.VMEM((count, half, width), jnp.float32),
            pltpu.VMEM((count - 1, half, width), jnp.float32),
            pltpu.SemaphoreType.DMA((count,)),
            dma(count), dma(count - 1), dma(count - 1), dma(count),
        ],
        compiler_params=params(tag),
    )(q3, inputs, out_grads, error)


def right_call(group, pairs, replicas, rank, p, p3, inputs, out_grads, error):
    rows, columns = error.shape[1:]
    count, half = group.count, rank // 2
    height, width = half // count, BLOCK
    blocks = columns // width
    others = count - 1
    return pl.pallas_call(
        functools.partial(right_kernel, group, pairs, replicas),
        name="right_reduce",
        out_shape=(
            jax.ShapeDtypeStruct((rank, columns), jnp.float32),
            jax.ShapeDtypeStruct((PIECES * rank, columns), jnp.bfloat16),
            jax.ShapeDtypeStruct(p.shape, jnp.float32),
        ),
        in_specs=[pl.BlockSpec(memory_space=pltpu.VMEM)] + in_places(),
        out_specs=[pl.BlockSpec(memory_space=pltpu.VMEM)] * 3,
        scratch_shapes=[
            pltpu.VMEM((rows, columns), jnp.bfloat16),
            pltpu.VMEM((rank, columns), jnp.float32),
            pltpu.VMEM((half, columns), jnp.float32),
            pltpu.VMEM((rank, columns), jnp.float32),
            pltpu.VMEM((blocks, half, width), jnp.float32),
            pltpu.VMEM((others, height, columns), jnp.float32),
            pltpu.VMEM((rank, 2 * rank), jnp.float32),
            pltpu.VMEM((pairs - 1, rank, 2 * rank), jnp.float32),
            pltpu.VMEM((rank, 2 * rank), jnp.float32),
            pltpu.VMEM((rank, 2 * rank), jnp.float32),
            pltpu.SemaphoreType.DMA((blocks,)),
            dma(blocks), dma(blocks * others), dma(others), dma(count), dma(pairs - 1),
        ],
        compiler_params=params(ITERS),
    )(p, p3, inputs, out_grads, error)


def rounded_pieces(value):
    pieces = []
    for _ in range(PIECES):
        piece = lax.reduce_precision(value, 8, 7)
        pieces.append(piece.astype(jnp.bfloat16))
        value = value - piece
    return jnp.concatenate(pieces, axis=0)


def plain_left(replicas, rank, a, q3, inputs, out_grads):
    inner = fold(contract(q3, out_grads, 1, 1), rank)
    outer = fold(contract(rounded_pieces(inner), inputs, 1, 0), rank)
    p = lax.psum((outer + fold(a, rank)) / replicas, ("rep", "fsdp"))
    return p, rounded_pieces(p)


def plain_right(replicas, rank, a, p, p3, inputs, out_grads):
    inner = fold(contract(p3, inputs, 1, 1), rank)
    outer = fold(contract(rounded_pieces(inner), out_grads, 1, 0), rank)
    q = lax.psum((outer + fold(a, rank)) / replicas, ("rep", "tp"))
    gram = lax.psum(contract(p, p, 1, 1, exact_mode), "tp")
    inverse = jax.scipy.linalg.solve_triangular(
        jnp.linalg.cholesky(gram), jnp.eye(rank, dtype=jnp.float32), lower=True
    )
    q = contract(inverse, q, 1, 0, exact_mode)
    return q, rounded_pieces(q), contract(inverse, p, 1, 0, exact_mode)


def shards(inputs, out_grads, error, q_init):
    replicas, splits, pairs = lax.axis_size("rep"), lax.axis_size("fsdp"), lax.axis_size("tp")
    rank = q_init.shape[1]
    rows, columns = error.shape[1:]
    left_group = Group("fsdp", replicas, splits)
    right_group = Group("tp", replicas, pairs)
    paired = replicas % 2 == 0 and rank == 64
    own_left = paired and left_group.count > 1 and rows % (left_group.count * 128) == 0
    own_right = (
        paired and pairs > 1 and rank % (right_group.count * 16) == 0 and columns % BLOCK == 0
    )
    q3 = q_init.T
    for iteration in range(ITERS):
        if own_left:
            p, p3 = left_call(iteration, left_group, replicas, rank, q3, inputs, out_grads, error)
        else:
            a = contract(q3, error[0], 1, 1)
            p, p3 = plain_left(replicas, rank, a, q3, inputs, out_grads)
        if own_right:
            q, q3, basis = right_call(
                right_group, pairs, replicas, rank, p, p3, inputs, out_grads, error
            )
        else:
            a = contract(p3, error[0], 1, 0)
            q, q3, basis = plain_right(replicas, rank, a, p, p3, inputs, out_grads)
    basis3 = rounded_pieces(-basis)
    high, low = basis3[:rank], basis3[rank : 2 * rank]
    lefts = jnp.concatenate([inputs, high, high, low], axis=0)
    rights = jnp.concatenate([out_grads, q3[:rank], q3[rank : 2 * rank], q3[:rank]], axis=0)
    merged = contract(lefts, rights, 0, 0) + error[0].astype(jnp.float32)
    p_factor = (basis * math.sqrt(rows * pairs)).astype(jnp.bfloat16).T
    return (merged.astype(jnp.bfloat16)[None], p_factor, q.astype(jnp.bfloat16).T)


def solution(mesh):
    in_specs = (P("rep", "tp"), P("rep", "fsdp"), P("rep", "tp", "fsdp"), P("fsdp", None))
    out_specs = (P("rep", "tp", "fsdp"), P("tp", None), P("fsdp", None))
    return jax.shard_map(shards, mesh=mesh, in_specs=in_specs, out_specs=out_specs, check_vma=False)
```

time: 170 us -> 127 us (0.75)
  matrix products: 46.1 us -> 14.2 us
  Pallas kernels: 122 us -> 107 us
  other arithmetic: 1.64 us -> 4.01 us
    dot_general x5 -> x1, matrix products: 46.1 us -> 14.2 us  [contract(): lax.dot_general(left, right, (((at_left,), (at_right,)), ((), ())), preci...]
    pallas_call x2, Pallas kernels: 63.6 us -> 54.4 us  [left_call(): pl.pallas_call(functools.partial(left_kernel, group, replicas), name='lef...]
    pallas_call x2, Pallas kernels: 58.1 us -> 52.9 us  [right_call(): pl.pallas_call(functools.partial(right_kernel, group, pairs, replicas), n...]
where the time goes in v2:
time: 127 us; the launch traced here: 126 us
  Pallas kernels  107 us (84%)
  matrix products  14.2 us (11%)
  other arithmetic  4.01 us (3%)
    pallas_call x2, Pallas kernels, left_call(): pl.pallas_call(functools.partial(left_kernel, group, replicas), name='lef...  54.4 us
    pallas_call x2, Pallas kernels, right_call(): pl.pallas_call(functools.partial(right_kernel, group, pairs, replicas), n...  52.9 us
    dot_general x1, matrix products, contract(): lax.dot_general(left, right, (((at_left,), (at_right,)), ((), ())), preci...  14.2 us

profile of v2, /device:TPU:0, one launch (start us, length us, event | category | flops | bytes accessed | tf_op | source)
XLA Modules:
  0.0 126.3 jit_solution(15607345034127262615)
XLA Ops:
  0.6 28.2 %left_reduce.2 = (f32[64,2048]{1,0:T(8,128)}, bf16[192,2048]{1,0:T(8,128)(2,1)}) custom-call(bf16[64,3584]{1,0:T(8,128)(2,1)} %bitcast.12, bf16[128,2048]{1,0:T(8,128)(2,1)} %x_ref.7, bf16[128,3584]{1,0:T(8,128)(2,1)} %g_ref.7, bf16[1,2048,3584]{2,1,0:T(8,128)(2,1)} %e_ref.7), custom_call_target="tpu_custom_call" | custom-call | tf_op jit(solution)/shard_map/left_reduce/pallas_call | solution.py:281
  28.8 27.0 %right_reduce.2 = (f32[64,3584]{1,0:T(8,128)}, bf16[192,3584]{1,0:T(8,128)(2,1)}, f32[64,2048]{1,0:T(8,128)}) custom-call(f32[64,2048]{1,0:T(8,128)} %get-tuple-element.11.p_ref, bf16[192,2048]{1,0:T(8,128)(2,1)} %get-tuple-element.12.p3_ref, bf16[128,2048]{1,0:T(8,128)(2,1)} %x_ref.7, bf16[128,3584]{1,0:T(8,128)(2,1)} %g_ref.7, bf16[1,2048,3584]{2,1,0:T(8,128)(2,1)} %e_ref.7), custom_call_target="tpu_custom_call" | custom-call | tf_op jit(solution)/shard_map/right_reduce/pallas_call | solution.py:309
  55.8 26.2 %left_reduce.3 = (f32[64,2048]{1,0:T(8,128)}, bf16[192,2048]{1,0:T(8,128)(2,1)}) custom-call(bf16[192,3584]{1,0:T(8,128)(2,1)} %get-tuple-element.13.q_ref, bf16[128,2048]{1,0:T(8,128)(2,1)} %x_ref.7, bf16[128,3584]{1,0:T(8,128)(2,1)} %g_ref.7, bf16[1,2048,3584]{2,1,0:T(8,128)(2,1)} %e_ref.7), custom_call_target="tpu_custom_call" | custom-call | tf_op jit(solution)/shard_map/left_reduce/pallas_call | solution.py:281
  82.0 25.9 %right_reduce.3 = (f32[64,3584]{1,0:T(8,128)}, bf16[192,3584]{1,0:T(8,128)(2,1)}, f32[64,2048]{1,0:T(8,128)}) custom-call(f32[64,2048]{1,0:T(8,128)} %get-tuple-element.14.p_ref, bf16[192,2048]{1,0:T(8,128)(2,1)} %get-tuple-element.15.p3_ref, bf16[128,2048]{1,0:T(8,128)(2,1)} %x_ref.7, bf16[128,3584]{1,0:T(8,128)(2,1)} %g_ref.7, bf16[1,2048,3584]{2,1,0:T(8,128)(2,1)} %e_ref.7), custom_call_target="tpu_custom_call" | custom-call | tf_op jit(solution)/shard_map/right_reduce/pallas_call | solution.py:309
  107.9 0.0 copy-start.2
  108.0 0.0 copy-start
  108.0 0.0 copy-start.1
  108.0 2.0 %fusion.16 = (bf16[2048,64]{0,1:T(8,128)(2,1)}, bf16[64,2048]{1,0:T(8,128)(2,1)S(1)}, bf16[64,2048]{1,0:T(8,128)(2,1)S(1)}) fusion(f32[64,2048]{1,0:T(8,128)} %get-tuple-element.16), kind=kLoop, calls=%fused_computation.21 | loop fusion | flops 1048576 | bytes 1310720 | tf_op jit(solution)/shard_map/transpose | solution.py:395
  110.0 2.0 %convert_bitcast_fusion = bf16[3584,64]{0,1:T(8,128)(2,1)} fusion(f32[64,3584]{1,0:T(8,128)} %get-tuple-element.18), kind=kLoop, calls=%fused_computation.20 | loop fusion | flops 229376 | bytes 1376256 | tf_op jit(solution)/shard_map/transpose | solution.py:396
  112.0 0.0 copy-done.2
  112.0 0.1 slice.8
  112.1 0.0 copy-done
  112.1 0.0 copy-done.1
  112.1 14.2 %fusion.1 = bf16[1,2048,3584]{2,1,0:T(8,128)(2,1)} fusion(bf16[1,2048,3584]{2,1,0:T(8,128)(2,1)} %e_ref.7, bf16[64,3584]{1,0:T(8,128)(2,1)S(1)} %slice.9, bf16[128,3584]{1,0:T(8,128)(2,1)S(1)} %slice.8, bf16[128,3584]{1,0:T(8,128)(2,1)S(1)} %copy-done, bf16[64,2048]{1,0:T(8,128)(2,1)S(1)} %get-tuple-element.20, bf16[64,2048]{1,0:T(8,128)(2,1)S(1)} %get-tuple-element.21, ...), kind=kOutput, calls=%fused_computation.2 | convolution fusion | flops 4731764736 | bytes 32702464 | tf_op jit(solution)/shard_map/dot_general | solution.py:19
  (1 shorter events, 0.0 us)
Async XLA Ops:
  107.9 4.1 %copy-start.2 = (bf16[192,3584]{1,0:T(8,128)(2,1)S(1)}, bf16[192,3584]{1,0:T(8,128)(2,1)}, u32[]{:S(2)}) copy-start(bf16[192,3584]{1,0:T(8,128)(2,1)} %get-tuple-element.17) | copy-start | bytes 4128772
  108.0 4.1 %copy-start = (bf16[128,3584]{1,0:T(8,128)(2,1)S(1)}, bf16[128,3584]{1,0:T(8,128)(2,1)}, u32[]{:S(2)}) copy-start(bf16[128,3584]{1,0:T(8,128)(2,1)} %g_ref.7) | copy-start | bytes 2752516
  108.0 4.1 %copy-start.1 = (bf16[128,2048]{1,0:T(8,128)(2,1)S(1)}, bf16[128,2048]{1,0:T(8,128)(2,1)}, u32[]{:S(2)}) copy-start(bf16[128,2048]{1,0:T(8,128)(2,1)} %x_ref.7) | copy-start | bytes 1572868

commit v3 on v2

--- a/solution.py
+++ b/solution.py
@@ -11,6 +11,7 @@
 ITERS = 2
 PIECES = 3
 BLOCK = 512
+HEIGHT = 256
 exact_mode = lax.Precision.HIGHEST
 MESH = pl.DeviceIdType.MESH
 
@@ -45,6 +46,7 @@
     def __init__(self, axis, replicas, size):
         self.axis, self.size = axis, size
         self.count = (replicas // 2) * size
+        self.wait_for = self.count
 
     def core(self):
         return lax.rem(lax.axis_index("rep"), 2)
@@ -69,7 +71,7 @@
             pl.semaphore_signal(barrier, inc=1, device_id=self.device(step), device_id_type=MESH)
 
     def meet(self):
-        pl.semaphore_wait(pltpu.get_barrier_semaphore(), self.count)
+        pl.semaphore_wait(pltpu.get_barrier_semaphore(), self.wait_for)
 
 
 def push(source, target, sems, at, device):
@@ -104,23 +106,18 @@
     return finish
 
 
-def left_kernel(group, replicas, q_ref, x_ref, g_ref, e_ref, p_ref, p3_ref,
-                held, total, outgoing, core_slots, slots,
-                load_sems, core_sems, send_sems, share_sems, pass_sems):
+def left_phase(group, replicas, loads, q_ref, x_ref, g_ref, p3_ref, held,
+               p_ref, total, outgoing, core_slots, slots,
+               core_sems, send_sems, share_sems, pass_sems):
     rank, columns = p_ref.shape
     count = group.count
     width, half = columns // count, rank // 2
     mine_rows, other_rows = aligned(group.core(), half), aligned(1 - group.core(), half)
     order = list(range(1, count)) + [0]
-    loads = {}
-    for step in order:
-        rows = aligned(group.at(step), width)
-        loads[step] = pltpu.make_async_copy(e_ref.at[0, rows, :], held.at[rows, :], load_sems.at[step])
-        loads[step].start()
-    group.greet()
     inner = fold(contract(q_ref[...], g_ref[...], 1, 1), rank)
     total[...] = fold(contract(pieces_of(inner), x_ref[...], 1, 0), rank)
-    group.meet()
+    if loads is not None:
+        group.meet()
     core_copies, copies = {}, []
 
     def forward(step):
@@ -135,7 +132,8 @@
 
     for place, step in enumerate(order):
         span = aligned(group.at(step), width)
-        loads[step].wait()
+        if loads is not None:
+            loads[step].wait()
         product = fold(contract(q_ref[...], held[span, :], 1, 1), rank)
         total[:, span] = (total[:, span] + product) / replicas
         core_copies[step] = push(
@@ -177,28 +175,18 @@
     lax.fori_loop(0, rank, eliminate, 0)
 
 
-def right_kernel(group, pairs, replicas, p_ref, p3_ref, x_ref, g_ref, e_ref,
-                 q_ref, q3_ref, basis_ref,
-                 held, total, summed, gathered, core_slots, slots, own_gram, gram_slots, grid, inverse,
-                 load_sems, core_sems, send_sems, share_sems, pass_sems, gram_sems):
-    rank, columns = q_ref.shape
+def right_phase(group, pairs, replicas, p_ref, p3_ref, x_ref, g_ref, q3_ref, basis_ref, held,
+                total, summed, gathered, core_slots, slots, own_gram, gram_slots, grid, inverse,
+                core_sems, send_sems, share_sems, pass_sems, gram_sems):
+    rank, columns = total.shape
     count = group.count
     half, height = rank // 2, rank // 2 // count
     blocks, _, width = core_slots.shape
     mine_rows, other_rows = aligned(group.core(), half), aligned(1 - group.core(), half)
-    loads = []
-    for block in range(blocks):
-        span = pl.ds(block * width, width)
-        loads.append(
-            pltpu.make_async_copy(e_ref.at[0, :, span], held.at[:, span], load_sems.at[block])
-        )
-        loads[-1].start()
-    group.greet()
     inner = fold(contract(p3_ref[...], x_ref[...], 1, 1), rank)
     total[...] = fold(contract(pieces_of(inner), g_ref[...], 1, 0), rank)
     left = p_ref[...]
     own_gram[...] = contract(left, jnp.concatenate([left, left], axis=0), 1, 1, exact_mode)
-    group.meet()
     gram_copies = []
     for step in range(1, pairs):
         target = lax.rem(lax.axis_index("tp") + step, pairs)
@@ -224,7 +212,6 @@
 
     for block in range(blocks):
         span = pl.ds(block * width, width)
-        loads[block].wait()
         product = fold(contract(p3_ref[...], held[:, span], 1, 0), rank)
         total[:, span] = (total[:, span] + product) / replicas
         core_copies.append(
@@ -253,85 +240,141 @@
     finish = gather(group, own_part, share_sems, pass_sems)
     invert_into(grid, inverse)
     lower = inverse[:, :rank]
-    basis_ref[...] = contract(lower, left, 1, 0, exact_mode)
+    if basis_ref is not None:
+        basis_ref[...] = contract(lower, left, 1, 0, exact_mode)
     for copy in copies + core_copies:
         copy.wait_send()
     finish()
-    result = contract(lower, gathered[...], 1, 0, exact_mode)
-    q_ref[...] = result
-    q3_ref[...] = pieces_of(result)
-
-
-def in_places():
-    return [pl.BlockSpec(memory_space=pltpu.VMEM)] * 3 + [pl.BlockSpec(memory_space=pl.ANY)]
+    q3_ref[...] = pieces_of(contract(lower, gathered[...], 1, 0, exact_mode))
+
+
+LEFT_REFS, RIGHT_REFS = 9, 14
+
+
+def factor_kernel(left_group, right_group, pairs, replicas, q_ref, x_ref, g_ref, e_ref,
+                  q3_ref, basis_ref, held, p3_ref, load_sems, *refs):
+    columns = held.shape[0]
+    count = left_group.count
+    width = columns // count
+    loads = {}
+    for step in list(range(1, count)) + [0]:
+        rows = aligned(left_group.at(step), width)
+        loads[step] = pltpu.make_async_copy(e_ref.at[0, rows, :], held.at[rows, :], load_sems.at[step])
+        loads[step].start()
+    barrier = pltpu.get_barrier_semaphore()
+    left_group.greet()
+    for step in range(1, right_group.count):
+        pl.semaphore_signal(barrier, inc=1, device_id=right_group.device(step), device_id_type=MESH)
+    left_group.wait_for = left_group.count + right_group.count - 1
+    for iteration in range(ITERS):
+        left, refs = refs[:LEFT_REFS], refs[LEFT_REFS:]
+        right, refs = refs[:RIGHT_REFS], refs[RIGHT_REFS:]
+        left_phase(
+            left_group, replicas, None if iteration else loads,
+            q3_ref if iteration else q_ref, x_ref, g_ref, p3_ref, held, *left,
+        )
+        right_phase(
+            right_group, pairs, replicas, left[0], p3_ref, x_ref, g_ref, q3_ref,
+            basis_ref if iteration == ITERS - 1 else None, held, *right,
+        )
 
 
 def dma(count):
     return pltpu.SemaphoreType.DMA((2, count))
 
 
-def params(tag):
-    return pltpu.CompilerParams(collective_id=tag, has_side_effects=True, vmem_limit_bytes=58 << 20)
-
-
-def left_call(tag, group, replicas, rank, q3, inputs, out_grads, error):
+def f32(*shape):
+    return pltpu.VMEM(shape, jnp.float32)
+
+
+def factor_call(left_group, right_group, pairs, replicas, rank, q3, inputs, out_grads, error):
     rows, columns = error.shape[1:]
-    count, half = group.count, rank // 2
-    width = rows // count
+    half = rank // 2
+    n, m = left_group.count, right_group.count
+    width, height, blocks = rows // n, half // m, columns // BLOCK
+    left = [
+        f32(rank, rows), f32(rank, rows), f32(n - 1, half, width), f32(n, half, width),
+        f32(n - 1, half, width), dma(n), dma(n - 1), dma(n - 1), dma(n),
+    ]
+    square = (rank, 2 * rank)
+    right = [
+        f32(rank, columns), f32(half, columns), f32(rank, columns), f32(blocks, half, BLOCK),
+        f32(m - 1, height, columns), f32(*square), f32(pairs - 1, *square), f32(*square),
+        f32(*square), dma(blocks), dma(blocks * (m - 1)), dma(m - 1), dma(m), dma(pairs - 1),
+    ]
+    vmem = pl.BlockSpec(memory_space=pltpu.VMEM)
     return pl.pallas_call(
-        functools.partial(left_kernel, group, replicas),
-        name="left_reduce",
+        functools.partial(factor_kernel, left_group, right_group, pairs, replicas),
+        name="factors",
         out_shape=(
+            jax.ShapeDtypeStruct((PIECES * rank, columns), jnp.bfloat16),
             jax.ShapeDtypeStruct((rank, rows), jnp.float32),
-            jax.ShapeDtypeStruct((PIECES * rank, rows), jnp.bfloat16),
         ),
-        in_specs=in_places(),
-        out_specs=[pl.BlockSpec(memory_space=pltpu.VMEM)] * 2,
+        in_specs=[vmem, vmem, vmem, pl.BlockSpec(memory_space=pl.ANY)],
+        out_specs=[vmem, vmem],
         scratch_shapes=[
             pltpu.VMEM((rows, columns), jnp.bfloat16),
-            pltpu.VMEM((rank, rows), jnp.float32),
-            pltpu.VMEM((count - 1, half, width), jnp.float32),
-            pltpu.VMEM((count, half, width), jnp.float32),
-            pltpu.VMEM((count - 1, half, width), jnp.float32),
-            pltpu.SemaphoreType.DMA((count,)),
-            dma(count), dma(count - 1), dma(count - 1), dma(count),
+            pltpu.VMEM((PIECES * rank, rows), jnp.bfloat16),
+            pltpu.SemaphoreType.DMA((n,)),
+        ]
+        + (left + right) * ITERS,
+        compiler_params=pltpu.CompilerParams(
+            collective_id=0, has_side_effects=True, vmem_limit_bytes=58 << 20
+        ),
+    )(q3, inputs, out_grads, error)
+
+
+def residual_kernel(scale, x_ref, g_ref, q3_ref, basis_ref, e_ref,
+                    error_ref, p_ref, q_ref, lefts, rights):
+    rank = basis_ref.shape[0]
+    height, columns = e_ref.shape[1:]
+    step = pl.program_id(0)
+
+    @pl.when(step == 0)
+    def _():
+        basis = basis_ref[...]
+        pieces = pieces_of(-basis)
+        high, low = pieces[:rank], pieces[rank : 2 * rank]
+        lefts[...] = jnp.concatenate([x_ref[...], high, high, low], axis=0)
+        q_high, q_low = q3_ref[:rank], q3_ref[rank : 2 * rank]
+        rights[...] = jnp.concatenate([g_ref[...], q_high, q_low, q_high], axis=0)
+        p_ref[...] = (basis * scale).astype(jnp.bfloat16)
+        q_ref[...] = q_high
+
+    left = lefts[:, aligned(step, height)].T
+    for at in range(0, columns, BLOCK):
+        span = pl.ds(at, BLOCK)
+        merged = contract(left, rights[:, span], 1, 0) + e_ref[0, :, span].astype(jnp.float32)
+        error_ref[0, :, span] = merged.astype(jnp.bfloat16)
+
+
+def residual_call(pairs, q3, basis, inputs, out_grads, error):
+    rank = basis.shape[0]
+    rows, columns = error.shape[1:]
+    depth = inputs.shape[0] + 3 * rank
+    height = HEIGHT
+
+    def fixed(shape):
+        return pl.BlockSpec(shape, lambda step: (0, 0))
+
+    block = pl.BlockSpec((1, height, columns), lambda step: (0, step, 0))
+    return pl.pallas_call(
+        functools.partial(residual_kernel, math.sqrt(rows * pairs)),
+        name="residual",
+        grid=(rows // height,),
+        out_shape=(
+            jax.ShapeDtypeStruct(error.shape, jnp.bfloat16),
+            jax.ShapeDtypeStruct((rank, rows), jnp.bfloat16),
+            jax.ShapeDtypeStruct((rank, columns), jnp.bfloat16),
+        ),
+        in_specs=[fixed(v.shape) for v in (inputs, out_grads, q3, basis)] + [block],
+        out_specs=[block, fixed((rank, rows)), fixed((rank, columns))],
+        scratch_shapes=[
+            pltpu.VMEM((depth, rows), jnp.bfloat16),
+            pltpu.VMEM((depth, columns), jnp.bfloat16),
         ],
-        compiler_params=params(tag),
-    )(q3, inputs, out_grads, error)
-
-
-def right_call(group, pairs, replicas, rank, p, p3, inputs, out_grads, error):
-    rows, columns = error.shape[1:]
-    count, half = group.count, rank // 2
-    height, width = half // count, BLOCK
-    blocks = columns // width
-    others = count - 1
-    return pl.pallas_call(
-        functools.partial(right_kernel, group, pairs, replicas),
-        name="right_reduce",
-        out_shape=(
-            jax.ShapeDtypeStruct((rank, columns), jnp.float32),
-            jax.ShapeDtypeStruct((PIECES * rank, columns), jnp.bfloat16),
-            jax.ShapeDtypeStruct(p.shape, jnp.float32),
-        ),
-        in_specs=[pl.BlockSpec(memory_space=pltpu.VMEM)] + in_places(),
-        out_specs=[pl.BlockSpec(memory_space=pltpu.VMEM)] * 3,
-        scratch_shapes=[
-            pltpu.VMEM((rows, columns), jnp.bfloat16),
-            pltpu.VMEM((rank, columns), jnp.float32),
-            pltpu.VMEM((half, columns), jnp.float32),
-            pltpu.VMEM((rank, columns), jnp.float32),
-            pltpu.VMEM((blocks, half, width), jnp.float32),
-            pltpu.VMEM((others, height, columns), jnp.float32),
-            pltpu.VMEM((rank, 2 * rank), jnp.float32),
-            pltpu.VMEM((pairs - 1, rank, 2 * rank), jnp.float32),
-            pltpu.VMEM((rank, 2 * rank), jnp.float32),
-            pltpu.VMEM((rank, 2 * rank), jnp.float32),
-            pltpu.SemaphoreType.DMA((blocks,)),
-            dma(blocks), dma(blocks * others), dma(others), dma(count), dma(pairs - 1),
-        ],
-        compiler_params=params(ITERS),
-    )(p, p3, inputs, out_grads, error)
+        compiler_params=pltpu.CompilerParams(vmem_limit_bytes=40 << 20),
+    )(inputs, out_grads, q3, basis, error)
 
 
 def rounded_pieces(value):
@@ -368,25 +411,24 @@
     rows, columns = error.shape[1:]
     left_group = Group("fsdp", replicas, splits)
     right_group = Group("tp", replicas, pairs)
-    paired = replicas % 2 == 0 and rank == 64
-    own_left = paired and left_group.count > 1 and rows % (left_group.count * 128) == 0
-    own_right = (
-        paired and pairs > 1 and rank % (right_group.count * 16) == 0 and columns % BLOCK == 0
-    )
+    if (
+        replicas % 2 == 0 and rank == 64 and pairs > 1 and left_group.count > 1
+        and rows % (left_group.count * 128) == 0 and rows % HEIGHT == 0
+        and rank % (right_group.count * 16) == 0 and columns % BLOCK == 0
+    ):
+        q3, basis = factor_call(
+            left_group, right_group, pairs, replicas, rank, q_init.T, inputs, out_grads, error
+        )
+        new_error, p_factor, q_factor = residual_call(
+            pairs, q3, basis, inputs, out_grads, error
+        )
+        return (new_error, p_factor.T, q_factor.T)
     q3 = q_init.T
-    for iteration in range(ITERS):
-        if own_left:
-            p, p3 = left_call(iteration, left_group, replicas, rank, q3, inputs, out_grads, error)
-        else:
-            a = contract(q3, error[0], 1, 1)
-            p, p3 = plain_left(replicas, rank, a, q3, inputs, out_grads)
-        if own_right:
-            q, q3, basis = right_call(
-                right_group, pairs, replicas, rank, p, p3, inputs, out_grads, error
-            )
-        else:
-            a = contract(p3, error[0], 1, 0)
-            q, q3, basis = plain_right(replicas, rank, a, p, p3, inputs, out_grads)
+    for _ in range(ITERS):
+        a = contract(q3, error[0], 1, 1)
+        p, p3 = plain_left(replicas, rank, a, q3, inputs, out_grads)
+        a = contract(p3, error[0], 1, 0)
+        q, q3, basis = plain_right(replicas, rank, a, p, p3, inputs, out_grads)
     basis3 = rounded_pieces(-basis)
     high, low = basis3[:rank], basis3[rank : 2 * rank]
     lefts = jnp.concatenate([inputs, high, high, low], axis=0)

time: 127 us -> 116 us (0.913)
  matrix products: 14.2 us -> 0 us
  Pallas kernels: 107 us -> 113 us
  other arithmetic: 4.01 us -> 0 us
  local copies, waits for them, and re-layouts: 0.11 us -> 2.38 us
    dot_general x1 -> x0, matrix products: 14.2 us -> none  [contract(): lax.dot_general(left, right, (((at_left,), (at_right,)), ((), ())), preci...]
    pallas_call x4 -> x2, Pallas kernels: 107 us -> 113 us  [the longest x1 97 us: factor_call(): pl.pallas_call(functools.partial(factor_kernel, left_group, right_group,...]
    transpose x2 -> x0, other arithmetic: 4.01 us -> none  [the longest x1 2.02 us: shards(): p_factor = (basis * math.sqrt(rows * pairs)).astype(jnp.bfloat16).T]
    unnamed x6 -> x8, local copies, waits for them, and re-layouts: 0.02 us -> 2.38 us
where the time goes in v3:
time: 116 us
  Pallas kernels  113 us (97%)
  local copies, waits for them, and re-layouts  2.38 us (2%)
    pallas_call x1, Pallas kernels, factor_call(): pl.pallas_call(functools.partial(factor_kernel, left_group, right_group,...  97 us
    pallas_call x1, Pallas kernels, residual_call(): pl.pallas_call(functools.partial(residual_kernel, math.sqrt(rows * pairs)...  15.8 us
    unnamed x8, local copies, waits for them, and re-layouts  2.38 us

profile of v3, /device:TPU:0, one launch (start us, length us, event | category | flops | bytes accessed | tf_op | source)
XLA Modules:
  0.0 115.9 jit_solution(12452736408203363355)
XLA Ops:
  0.6 0.0 copy-start
  0.6 0.0 copy-start.1
  0.7 97.0 %factors.1 = (bf16[192,3584]{1,0:T(8,128)(2,1)}, f32[64,2048]{1,0:T(8,128)}) custom-call(bf16[64,3584]{1,0:T(8,128)(2,1)} %bitcast.3, bf16[128,2048]{1,0:T(8,128)(2,1)} %x_ref.3, bf16[128,3584]{1,0:T(8,128)(2,1)} %g_ref.3, bf16[1,2048,3584]{2,1,0:T(8,128)(2,1)} %e_ref.3), custom_call_target="tpu_custom_call" | custom-call | tf_op jit(solution)/shard_map/factors/pallas_call | solution.py:306
  97.7 0.0 copy-done
  97.7 0.0 copy-done.1
  97.7 0.0 copy-start.2
  97.7 1.3 %copy-done.2 = bf16[192,3584]{1,0:T(8,128)(2,1)S(1)} copy-done((bf16[192,3584]{1,0:T(8,128)(2,1)S(1)}, bf16[192,3584]{1,0:T(8,128)(2,1)}, u32[]{:S(2)}) %copy-start.2) | copy-done | bytes 1376280
  99.1 0.0 copy-start.3
  99.1 1.0 copy-done.3
  100.1 15.8 %residual.1 = (bf16[1,2048,3584]{2,1,0:T(8,128)(2,1)}, bf16[64,2048]{1,0:T(8,128)(2,1)}, bf16[64,3584]{1,0:T(8,128)(2,1)}) custom-call(bf16[128,2048]{1,0:T(8,128)(2,1)S(1)} %copy-done.1, bf16[128,3584]{1,0:T(8,128)(2,1)S(1)} %copy-done, bf16[192,3584]{1,0:T(8,128)(2,1)S(1)} %copy-done.2, f32[64,2048]{1,0:T(8,128)S(1)} %copy-done.3, bf16[1,2048,3584]{2,1,0:T(8,128)(2,1)} %e_ref.3), custom_call_target="tpu_custom_call" | custom-call | tf_op jit(solution)/shard_map/residual/pallas_call | solution.py:361
Async XLA Ops:
  0.6 97.1 %copy-start = (bf16[128,3584]{1,0:T(8,128)(2,1)S(1)}, bf16[128,3584]{1,0:T(8,128)(2,1)}, u32[]{:S(2)}) copy-start(bf16[128,3584]{1,0:T(8,128)(2,1)} %g_ref.3) | copy-start | bytes 2752516
  0.6 97.1 %copy-start.1 = (bf16[128,2048]{1,0:T(8,128)(2,1)S(1)}, bf16[128,2048]{1,0:T(8,128)(2,1)}, u32[]{:S(2)}) copy-start(bf16[128,2048]{1,0:T(8,128)(2,1)} %x_ref.3) | copy-start | bytes 1572868
  97.7 1.3 %copy-start.2 = (bf16[192,3584]{1,0:T(8,128)(2,1)S(1)}, bf16[192,3584]{1,0:T(8,128)(2,1)}, u32[]{:S(2)}) copy-start(bf16[192,3584]{1,0:T(8,128)(2,1)} %get-tuple-element.8.q3_ref) | copy-start | bytes 4128772
  99.1 1.0 copy-start.3

commit v4 on v3

--- a/solution.py
+++ b/solution.py
@@ -11,7 +11,7 @@
 ITERS = 2
 PIECES = 3
 BLOCK = 512
-HEIGHT = 256
+HEIGHT = 512
 exact_mode = lax.Precision.HIGHEST
 MESH = pl.DeviceIdType.MESH
 
@@ -33,6 +33,15 @@
         pieces.append(piece)
         value = value - piece.astype(jnp.float32)
     return jnp.concatenate(pieces, axis=0)
+
+
+def full_product(left, right):
+    turned, split = pieces_of(left.T), pieces_of(right)
+    rank = left.shape[1]
+    pairs = [(0, 0), (0, 1), (1, 0), (0, 2), (2, 0), (1, 1)]
+    lefts = [turned[a * rank : (a + 1) * rank] for a, _ in pairs]
+    rights = [split[b * rank : (b + 1) * rank] for _, b in pairs]
+    return contract(jnp.concatenate(lefts, axis=0), jnp.concatenate(rights, axis=0), 0, 0)
 
 
 def fold(stacked, rank):
@@ -241,11 +250,11 @@
     invert_into(grid, inverse)
     lower = inverse[:, :rank]
     if basis_ref is not None:
-        basis_ref[...] = contract(lower, left, 1, 0, exact_mode)
+        basis_ref[...] = full_product(lower, left)
     for copy in copies + core_copies:
         copy.wait_send()
     finish()
-    q3_ref[...] = pieces_of(contract(lower, gathered[...], 1, 0, exact_mode))
+    q3_ref[...] = pieces_of(full_product(lower, gathered[...]))
 
 
 LEFT_REFS, RIGHT_REFS = 9, 14
@@ -319,7 +328,7 @@
         ]
         + (left + right) * ITERS,
         compiler_params=pltpu.CompilerParams(
-            collective_id=0, has_side_effects=True, vmem_limit_bytes=58 << 20
+            collective_id=0, has_side_effects=True, vmem_limit_bytes=50 << 20
         ),
     )(q3, inputs, out_grads, error)
 

time: 116 us -> 113 us (0.974)
  Pallas kernels: 113 us -> 109 us
    pallas_call x1, Pallas kernels: 97 us -> 94 us  [factor_call(): pl.pallas_call(functools.partial(factor_kernel, left_group, right_group,...]
    unnamed x8 -> x6, local copies, waits for them, and re-layouts: 2.38 us -> 3.23 us
where the time goes in v4:
time: 113 us
  Pallas kernels  109 us (96%)
  local copies, waits for them, and re-layouts  3.23 us (3%)
    pallas_call x1, Pallas kernels, factor_call(): pl.pallas_call(functools.partial(factor_kernel, left_group, right_group,...  94 us
    pallas_call x1, Pallas kernels, residual_call(): pl.pallas_call(functools.partial(residual_kernel, math.sqrt(rows * pairs)...  14.7 us
    unnamed x6, local copies, waits for them, and re-layouts  3.23 us

profile of v4, /device:TPU:0, one launch (start us, length us, event | category | flops | bytes accessed | tf_op | source)
XLA Modules:
  0.0 112.5 jit_solution(8929524244305622140)
XLA Ops:
  0.6 0.0 copy-start
  0.6 1.2 %copy-done = bf16[128,3584]{1,0:T(8,128)(2,1)S(1)} copy-done((bf16[128,3584]{1,0:T(8,128)(2,1)S(1)}, bf16[128,3584]{1,0:T(8,128)(2,1)}, u32[]{:S(2)}) %copy-start) | copy-done | bytes 917528
  1.8 0.0 copy-start.1
  1.8 1.0 copy-done.1
  2.9 0.0 copy-start.2
  2.9 1.0 copy-done.2
  3.9 94.0 %factors.1 = (bf16[192,3584]{1,0:T(8,128)(2,1)S(1)}, f32[64,2048]{1,0:T(8,128)S(1)}) custom-call(bf16[64,3584]{1,0:T(8,128)(2,1)S(1)} %bitcast.3, bf16[128,2048]{1,0:T(8,128)(2,1)S(1)} %copy-done.1, bf16[128,3584]{1,0:T(8,128)(2,1)S(1)} %copy-done, bf16[1,2048,3584]{2,1,0:T(8,128)(2,1)} %e_ref.3), custom_call_target="tpu_custom_call" | custom-call | tf_op jit(solution)/shard_map/factors/pallas_call | solution.py:315
  97.9 14.7 %residual.1 = (bf16[1,2048,3584]{2,1,0:T(8,128)(2,1)}, bf16[64,2048]{1,0:T(8,128)(2,1)}, bf16[64,3584]{1,0:T(8,128)(2,1)}) custom-call(bf16[128,2048]{1,0:T(8,128)(2,1)S(1)} %copy-done.1, bf16[128,3584]{1,0:T(8,128)(2,1)S(1)} %copy-done, bf16[192,3584]{1,0:T(8,128)(2,1)S(1)} %get-tuple-element.8.q3_ref, f32[64,2048]{1,0:T(8,128)S(1)} %get-tuple-element.9.basis_ref, ...), custom_call_target="tpu_custom_call" | custom-call | tf_op jit(solution)/shard_map/residual/pallas_call | solution.py:370
Async XLA Ops:
  0.6 1.2 %copy-start = (bf16[128,3584]{1,0:T(8,128)(2,1)S(1)}, bf16[128,3584]{1,0:T(8,128)(2,1)}, u32[]{:S(2)}) copy-start(bf16[128,3584]{1,0:T(8,128)(2,1)} %g_ref.3) | copy-start | bytes 2752516
  1.8 1.0 copy-start.1
  2.9 1.0 copy-start.2
